TPU v7x, 256 devices: a whole 4x4x8 slice. The times are simulated.
256 devices in a mesh: sx: 8 (over z_hi, x), sy: 4 (over z_lo), af: 8 (over y, core).
Axes of the slice: x: 4, y: 4, z: 8 (z_hi: 2, z_lo: 4; z = z_hi * 4 + z_lo), core: 2. Of those that a mesh axis runs over, the one named last changes fastest.
Arguments:
- volume: bfloat16 [8, 48, 48, 48, 128], P('af', 'sx', 'sy'), may hold values from -6 to 6
- kernel: bfloat16 [3, 3, 3, 128, 256], P(None, None, None, 'sx', ('sy', 'af')), may hold values from -0.109375 to 0.109375
- cotangent: bfloat16 [8, 256, 24, 576], P('sx', ('sy', 'af')), may hold values from -6 to 6
Outputs:
- features: bfloat16 [8, 256, 24, 576], P('sx', ('sy', 'af'))
- volume_grad: bfloat16 [8, 48, 48, 48, 128], P('af', 'sx', 'sy')
- kernel_grad: float32 [3, 3, 3, 128, 256], P(None, None, None, 'sx', ('sy', 'af'))
All inputs are finite; a program needn't handle non-finite values.
Results may differ from a plain program's by a relative error of at most 0.0025.
Values may be sent and summed in bfloat16 or wider, within the bound.
A program may use at most 64 MiB of HBM per device.

v0:
```python
import functools

import jax
import jax.numpy as jnp
from jax import lax
from jax.experimental import pallas as pl
from jax.experimental.pallas import tpu as pltpu
from jax.sharding import PartitionSpec as P


def _gather_body(n_sy, n_af, block_ref, out_ref, send_sem, recv_sem):
    group = n_sy * n_af
    sx = lax.axis_index("sx")
    me = lax.axis_index("sy") * n_af + lax.axis_index("af")
    barrier = pltpu.get_barrier_semaphore()
    for step in range(1, group):
        peer = lax.rem(me + step, group)
        pl.semaphore_signal(
            barrier,
            inc=1,
            device_id=(sx, peer // n_af, lax.rem(peer, n_af)),
            device_id_type=pl.DeviceIdType.MESH,
        )
    pl.semaphore_wait(barrier, group - 1)
    copies = []
    for step in range(1, group):
        peer = lax.rem(me + step, group)
        copy = pltpu.make_async_remote_copy(
            src_ref=block_ref,
            dst_ref=out_ref.at[me],
            send_sem=send_sem.at[step - 1],
            recv_sem=recv_sem.at[step - 1],
            device_id=(sx, peer // n_af, lax.rem(peer, n_af)),
            device_id_type=pl.DeviceIdType.MESH,
        )
        copy.start()
        copies.append(copy)
    out_ref[me] = block_ref[...]
    for copy in copies:
        copy.wait_send()
    for step in range(1, group):
        source = lax.rem(me + group - step, group)
        incoming = pltpu.make_async_remote_copy(
            src_ref=block_ref,
            dst_ref=out_ref.at[source],
            send_sem=send_sem.at[step - 1],
            recv_sem=recv_sem.at[step - 1],
            device_id=(sx, source // n_af, lax.rem(source, n_af)),
            device_id_type=pl.DeviceIdType.MESH,
        )
        incoming.wait_recv()


def _reduce_body(n_sy, n_af, terms_ref, out_ref, from_sib, mine, held, sib_send, sib_recv, send_sem, recv_sem):
    half = n_sy * n_af // 2
    rows = out_ref.shape[0]
    span = half * rows
    sx = lax.axis_index("sx")
    sy = lax.axis_index("sy")
    af = lax.axis_index("af")
    parity = lax.rem(af, 2)
    sib_af = af + 1 - 2 * parity
    me = sy * (n_af // 2) + af // 2

    def peer_of(index):
        block = 2 * index + parity
        return (sx, block // n_af, lax.rem(block, n_af))

    barrier = pltpu.get_barrier_semaphore()
    pl.semaphore_signal(barrier, inc=1, device_id=(sx, sy, sib_af), device_id_type=pl.DeviceIdType.MESH)
    for step in range(1, half):
        pl.semaphore_signal(
            barrier,
            inc=1,
            device_id=peer_of(lax.rem(me + step, half)),
            device_id_type=pl.DeviceIdType.MESH,
        )
    pl.semaphore_wait(barrier, half)
    to_sib = pltpu.make_async_remote_copy(
        src_ref=terms_ref.at[pl.ds(pl.multiple_of((1 - parity) * span, span), span)],
        dst_ref=from_sib,
        send_sem=sib_send,
        recv_sem=sib_recv,
        device_id=(sx, sy, sib_af),
        device_id_type=pl.DeviceIdType.MESH,
    )
    to_sib.start()
    to_sib.wait_send()
    to_sib.wait_recv()
    mine[...] = terms_ref[pl.ds(pl.multiple_of(parity * span, span), span), :] + from_sib[...]
    copies = []
    for step in range(1, half):
        peer = lax.rem(me + step, half)
        copy = pltpu.make_async_remote_copy(
            src_ref=mine.at[pl.ds(pl.multiple_of(peer * rows, rows), rows)],
            dst_ref=held.at[me],
            send_sem=send_sem.at[step - 1],
            recv_sem=recv_sem.at[step - 1],
            device_id=peer_of(peer),
            device_id_type=pl.DeviceIdType.MESH,
        )
        copy.start()
        copies.append(copy)
    total = mine[pl.ds(pl.multiple_of(me * rows, rows), rows), :]
    for copy in copies:
        copy.wait_send()
    for step in range(1, half):
        source = lax.rem(me + half - step, half)
        incoming = pltpu.make_async_remote_copy(
            src_ref=mine.at[pl.ds(0, rows)],
            dst_ref=held.at[source],
            send_sem=send_sem.at[step - 1],
            recv_sem=recv_sem.at[step - 1],
            device_id=peer_of(source),
            device_id_type=pl.DeviceIdType.MESH,
        )
        incoming.wait_recv()
        total = total + held[source]
    out_ref[...] = total


def reduce_filters(terms):
    n_sy = lax.axis_size("sy")
    n_af = lax.axis_size("af")
    group = n_sy * n_af
    rows = terms.shape[0] // group
    return pl.pallas_call(
        functools.partial(_reduce_body, n_sy, n_af),
        out_shape=jax.ShapeDtypeStruct((rows, terms.shape[1]), terms.dtype),
        in_specs=[pl.BlockSpec(memory_space=pltpu.VMEM)],
        out_specs=pl.BlockSpec(memory_space=pltpu.VMEM),
        scratch_shapes=[
            pltpu.VMEM((group // 2 * rows, terms.shape[1]), terms.dtype),
            pltpu.VMEM((group // 2 * rows, terms.shape[1]), terms.dtype),
            pltpu.VMEM((group // 2, rows, terms.shape[1]), terms.dtype),
            pltpu.SemaphoreType.DMA(()),
            pltpu.SemaphoreType.DMA(()),
            pltpu.SemaphoreType.DMA((group // 2 - 1,)),
            pltpu.SemaphoreType.DMA((group // 2 - 1,)),
        ],
        compiler_params=pltpu.CompilerParams(collective_id=1, has_side_effects=True),
        cost_estimate=pl.CostEstimate(
            flops=terms.size, bytes_accessed=2 * terms.size * 4, transcendentals=0
        ),
    )(terms)


def gather_filters(kernel):
    n_sy = lax.axis_size("sy")
    n_af = lax.axis_size("af")
    group = n_sy * n_af
    taps, channels, per_dev = kernel.shape[0] * kernel.shape[1] * kernel.shape[2], kernel.shape[3], kernel.shape[4]
    block = kernel.reshape(-1, 128)
    gathered = pl.pallas_call(
        functools.partial(_gather_body, n_sy, n_af),
        out_shape=jax.ShapeDtypeStruct((group,) + block.shape, block.dtype),
        in_specs=[pl.BlockSpec(memory_space=pltpu.VMEM)],
        out_specs=pl.BlockSpec(memory_space=pltpu.VMEM),
        scratch_shapes=[
            pltpu.SemaphoreType.DMA((group - 1,)),
            pltpu.SemaphoreType.DMA((group - 1,)),
        ],
        compiler_params=pltpu.CompilerParams(collective_id=0, has_side_effects=True),
    )(block)
    gathered = gathered.reshape(group, taps, channels, per_dev).transpose(1, 2, 0, 3)
    return gathered.reshape(kernel.shape[:4] + (group * per_dev,))


def flat_all_to_all(x, axes):
    moved = lax.all_to_all(x.reshape(x.shape[0], 2, -1), axes, 0, 0, tiled=True)
    return moved.reshape(x.shape)


def from_behind(value, axis, steps):
    count = lax.axis_size(axis)
    leading, last = (max(0, -steps), min(count, count - steps))
    return lax.ppermute(value, axis, [(source, source + steps) for source in range(leading, last)])


def strided_patch(extended, tap_d, tap_h, tap_w, depth, height, width):
    return extended[
        :,
        tap_d : tap_d + 2 * depth : 2,
        tap_h : tap_h + 2 * height : 2,
        tap_w : tap_w + 2 * width : 2,
        :,
    ]


def parity_view(extended):
    samples, d_ext, h_ext, w_ext, channels = extended.shape
    pads = [(0, 0)] + [(0, n % 2) for n in (d_ext, h_ext, w_ext)] + [(0, 0)]
    even = jnp.pad(extended, pads)
    _, d2, h2, w2, _ = even.shape
    return even.reshape(samples, d2 // 2, 2, h2 // 2, 2, w2, channels)


def _im2col_body(depth, height, width, x_ref, out_ref):
    channels = x_ref.shape[-1]
    tap = 0
    for tap_d in range(3):
        for tap_h in range(3):
            for tap_w in range(3):
                od, oh = tap_d // 2, tap_h // 2
                for p in range(depth):
                    for q in range(height):
                        row = x_ref[0, od + p, tap_d % 2, oh + q, tap_h % 2, pl.ds(tap_w, width, stride=2), :]
                        out_ref[p, q, :, tap * channels : (tap + 1) * channels] = row.astype(out_ref.dtype)
                tap += 1


def im2col(classes, depth, height, width):
    channels = classes.shape[-1]
    return pl.pallas_call(
        functools.partial(_im2col_body, depth, height, width),
        out_shape=jax.ShapeDtypeStruct((depth, height, width, 27 * channels), classes.dtype),
        in_specs=[pl.BlockSpec(memory_space=pltpu.VMEM)],
        out_specs=pl.BlockSpec(memory_space=pltpu.VMEM),
    )(classes.astype(jnp.float32))


def weave(even_part, odd_part, axis):
    stacked = jnp.stack([even_part, odd_part], axis=axis + 1)
    shape = list(even_part.shape)
    shape[axis] = shape[axis] * 2
    return stacked.reshape(shape)


def spread_back(grad_t, kernel_full, samples, depth, height, width):
    filters = grad_t.shape[0]
    channels = kernel_full.shape[3]
    spread = lax.dot_general(
        grad_t,
        kernel_full.reshape(-1, channels, filters),
        (((0,), (2,)), ((), ())),
        preferred_element_type=jnp.float32,
    ).reshape(samples, depth, height, width, 27, channels)
    classes = {}
    for tap_d in range(3):
        for tap_h in range(3):
            for tap_w in range(3):
                term = spread[:, :, :, :, tap_d * 9 + tap_h * 3 + tap_w]
                pads = [(0, 0)]
                for tap in (tap_d, tap_h, tap_w):
                    pads.append((1, 0) if tap == 2 else (0, 1))
                pads.append((0, 0))
                term = jnp.pad(term, pads)
                key_name = (tap_d % 2, tap_h % 2, tap_w % 2)
                classes[key_name] = classes[key_name] + term if key_name in classes else term
    planes = []
    for parity_d in range(2):
        rows_h = []
        for parity_h in range(2):
            rows_h.append(weave(classes[parity_d, parity_h, 0], classes[parity_d, parity_h, 1], 3))
        planes.append(weave(rows_h[0], rows_h[1], 2))
    whole = weave(planes[0], planes[1], 1)
    return whole[:, : 2 * depth + 1, : 2 * height + 1, : 2 * width + 1, :]


def on_device(volume, kernel, cotangent):
    samples = volume.shape[0]
    depth = volume.shape[1] // 2
    height = volume.shape[2] // 2
    width = volume.shape[3] // 2
    n_sy = lax.axis_size("sy")
    n_af = lax.axis_size("af")
    kernel_part = gather_filters(kernel)
    kernel_full = lax.all_gather(kernel_part, "sx", axis=3, tiled=True)
    filters = kernel_full.shape[4]
    per_dev = filters // (n_sy * n_af)
    below = from_behind(volume[:, -1:], "sx", 1)
    n_sx_axis = lax.axis_size("sx")
    corner = lax.ppermute(
        volume[:, -1:, -1:],
        ("sx", "sy"),
        [
            (i * n_sy + j, (i + 1) * n_sy + j + 1)
            for i in range(n_sx_axis - 1)
            for j in range(n_sy - 1)
        ],
    )
    beside = jnp.concatenate([corner, from_behind(volume[:, :, -1:], "sy", 1)], axis=1)
    extended = jnp.concatenate([below, volume], axis=1)
    extended = jnp.concatenate([beside, extended], axis=2)
    extended = jnp.pad(extended, ((0, 0), (0, 0), (0, 0), (1, 0), (0, 0)))
    rows = samples * depth * height * width
    classes = parity_view(extended)
    cols = im2col(classes, depth, height, width).reshape(rows, -1)
    kernel_mat = kernel_full.reshape(-1, filters)
    total = lax.dot_general(
        kernel_mat, cols, (((0,), (1,)), ((), ())), preferred_element_type=jnp.float32
    )
    n_sx = lax.axis_size("sx")
    conv_t = total.astype(jnp.bfloat16).reshape(n_sy, n_af, per_dev, depth, height, width)
    by_af = flat_all_to_all(conv_t.transpose(1, 0, 2, 3, 4, 5), "af")
    by_region = by_af.reshape(n_sx * n_sy, per_dev, depth, height, width)
    gathered = flat_all_to_all(by_region, ("sx", "sy"))
    own_samples = cotangent.shape[0]
    features = (
        gathered.reshape(n_sx, n_sy, per_dev, depth, height, width)
        .transpose(2, 0, 3, 1, 4, 5)
        .reshape(cotangent.shape)
    )
    grad_blocks = (
        cotangent.reshape(per_dev, n_sx, depth, n_sy, height, width)
        .transpose(1, 3, 0, 2, 4, 5)
        .reshape(n_sx * n_sy, per_dev, depth, height, width)
    )
    grad_region = flat_all_to_all(grad_blocks, ("sx", "sy"))
    grad_region = grad_region.reshape(n_sx * own_samples, n_sy, per_dev, depth, height, width)
    grad_back = flat_all_to_all(grad_region, "af")
    grad_t = grad_back.transpose(1, 0, 2, 3, 4, 5).reshape(filters, rows)
    by_parity = grad_t.reshape(n_sy * n_af // 2, 2, per_dev, rows).transpose(1, 0, 2, 3)
    kernel_terms = lax.dot_general(
        by_parity.reshape(filters, rows), cols, (((1,), (0,)), ((), ())),
        preferred_element_type=jnp.float32,
    )
    channels = kernel_full.shape[3]
    own_ch = channels // n_sx
    by_filter = reduce_filters(kernel_terms)
    by_filter = by_filter.reshape(per_dev, 27, n_sx, own_ch).transpose(2, 1, 3, 0)
    kernel_grad = lax.all_to_all(by_filter, "sx", 0, 0, tiled=True).sum(axis=0)
    kernel_grad = kernel_grad.reshape(3, 3, 3, own_ch, per_dev)
    partial_grad = spread_back(grad_t, kernel_full, samples, depth, height, width)
    from_above = from_behind(partial_grad[:, 0:1], "sx", -1)
    own_depth = partial_grad[:, 1:]
    own_depth = jnp.concatenate([own_depth[:, :-1], own_depth[:, -1:] + from_above], axis=1)
    from_right = from_behind(own_depth[:, :, 0:1].astype(jnp.bfloat16), "sy", -1).astype(
        jnp.float32
    )
    own_height = own_depth[:, :, 1:]
    own_height = jnp.concatenate(
        [own_height[:, :, :-1], own_height[:, :, -1:] + from_right], axis=2
    )
    volume_grad = own_height[:, :, :, 1:]
    return (features, volume_grad.astype(jnp.bfloat16), kernel_grad)


def solution(mesh):
    return jax.shard_map(
        on_device,
        mesh=mesh,
        in_specs=(
            P("af", "sx", "sy", None, None),
            P(None, None, None, "sx", ("sy", "af")),
            P("sx", ("sy", "af"), None, None),
        ),
        out_specs=(
            P("sx", ("sy", "af"), None, None),
            P("af", "sx", "sy", None, None),
            P(None, None, None, "sx", ("sy", "af")),
        ),
        check_vma=False,
    )
```

profile of v0, /device:TPU:8, one launch (start us, length us, event | category | flops | bytes accessed | tf_op | source)
XLA Modules:
  0.0 214.3 jit_solution(6349167545733426325)
XLA Ops:
  7.2 0.9 copy.204
  8.1 0.7 reshape.77.block_ref
  8.9 14.3 %shard_map.59 = bf16[32,27,128]{2,1,0:T(8,128)(2,1)} custom-call(bf16[27,128]{1,0:T(8,128)(2,1)} %reshape.77.block_ref), custom_call_target="tpu_custom_call" | custom-call | tf_op jit(solution)/shard_map/pallas_call | solution.py:154
  23.2 1.4 copy.205
  24.6 2.1 copy.206
  26.7 1.3 copy.207
  28.1 2.2 %reshape.84 = bf16[8,8,3,4,6,24]{5,4,3,2,1,0:T(8,128)(2,1)S(1)} reshape(bf16[1,8,24,576]{3,2,1,0:T(8,128)(2,1)S(1)} %copy-done.5) | data formatting | bytes 442368 | tf_op jit(solution)/shard_map/reshape | solution.py:305
  30.8 2.2 %reshape_reshape.10 = bf16[32,2,1728]{2,1,0:T(2,128)(2,1)} reshape(bf16[8,4,8,3,6,24]{5,4,3,2,1,0:T(8,128)(2,1)S(1)} %copy.211) | data formatting | bytes 442368 | tf_op jit(solution)/shard_map/reshape;reshape | solution.py:170
  33.0 9.7 %all-to-all-start.2 = ((bf16[32,2,1728]{2,1,0:T(2,128)(2,1)}), bf16[32,2,1728]{2,1,0:T(2,128)(2,1)S(1)}, u32[]{:S(2)}, u32[]{:S(2)}) async-start(bf16[32,2,1728]{2,1,0:T(2,128)(2,1)} %reshape_reshape.10), calls=%async_computation.2 | async-start | bytes 458752 | tf_op jit(solution)/shard_map/all_to_all | solution.py:170
  42.7 3.7 %collective-permute-start.2 = (bf16[1,1,12,48,128]{4,3,2,1,0:T(8,128)(2,1)S(1)}, bf16[1,1,12,48,128]{4,3,2,1,0:T(8,128)(2,1)S(1)}, u32[]{:S(2)}, u32[]{:S(2)}) collective-permute-start(bf16[1,1,12,48,128]{4,3,2,1,0:T(8,128)(2,1)S(1)} %slice.125), channel_id=1, source_target_pairs={{0,32},{32,64},{64,96},{96,128},{128,160},{160,192},{192,224},{1,3... | collective-permute-start | bytes 442376 | tf_op jit(solution)/shard_map/ppermute | solution.py:177
  46.5 3.4 %collective-permute-start.1 = (bf16[1,6,1,48,128]{4,3,2,1,0:T(8,128)(2,1)S(1)}, bf16[1,6,1,48,128]{4,3,2,1,0:T(8,128)(2,1)S(1)}, u32[]{:S(2)}, u32[]{:S(2)}) collective-permute-start(bf16[1,6,1,48,128]{4,3,2,1,0:T(8,128)(2,1)S(1)} %slice.124), channel_id=1, source_target_pairs={{0,8},{8,16},{16,24},{1,9},{9,17},{17,25},{2,10},{10,18},{18,26},{... | collective-permute-start | bytes 221192 | tf_op jit(solution)/shard_map/ppermute | solution.py:177
  49.9 4.3 %collective-permute-start = (bf16[1,1,1,48,128]{4,3,2,1,0:T(8,128)(2,1)S(1)}, bf16[1,1,1,48,128]{4,3,2,1,0:T(8,128)(2,1)S(1)}, u32[]{:S(2)}, u32[]{:S(2)}) collective-permute-start(bf16[1,1,1,48,128]{4,3,2,1,0:T(8,128)(2,1)S(1)} %slice.123), channel_id=1, source_target_pairs={{0,40},{8,48},{16,56},{32,72},{40,80},{48,88},{64,104},{72,112},{8... | collective-permute-start | bytes 36872 | tf_op jit(solution)/shard_map/ppermute | solution.py:273
  54.1 6.0 %all-to-all-done.2 = bf16[32,2,1728]{2,1,0:T(2,128)(2,1)S(1)} async-done(((bf16[32,2,1728]{2,1,0:T(2,128)(2,1)}), bf16[32,2,1728]{2,1,0:T(2,128)(2,1)S(1)}, u32[]{:S(2)}, u32[]{:S(2)}) %all-to-all-start.2) | async-done | bytes 221216 | tf_op jit(solution)/shard_map/all_to_all | solution.py:170
  60.1 1.0 reshape_reshape_reshape.7
  61.1 5.7 %all-to-all-start.3 = ((bf16[8,2,6912]{2,1,0:T(2,128)(2,1)}), bf16[8,2,6912]{2,1,0:T(2,128)(2,1)S(1)}, u32[]{:S(2)}, u32[]{:S(2)}) async-start(bf16[8,2,6912]{2,1,0:T(2,128)(2,1)} %reshape_reshape_reshape.7), calls=%async_computation.3 | async-start | bytes 442368 | tf_op jit(solution)/shard_map/all_to_all | solution.py:170
  67.5 1.9 convert.12.x_ref
  69.5 4.1 %shard_map.58 = bf16[3,6,24,3456]{3,2,1,0:T(8,128)(2,1)} custom-call(f32[1,4,2,7,2,50,128]{6,5,4,3,2,1,0:T(8,128)} %convert.12.x_ref), custom_call_target="tpu_custom_call" | custom-call | tf_op jit(solution)/shard_map/pallas_call | solution.py:214
  73.5 1.7 reshape.85
  75.6 0.9 reshape_reshape.11
  76.5 0.9 reshape.86
  77.5 4.7 %convolution_bitcast_fusion.terms_ref = f32[256,3456]{1,0:T(8,128)} fusion(bf16[256,432]{1,0:T(8,128)(2,1)S(1)} %bitcast.192, bf16[432,3456]{1,0:T(8,128)(2,1)} %bitcast.172), kind=kOutput, calls=%fused_computation | convolution fusion | flops 764411904 | bytes 6746112 | tf_op jit(solution)/shard_map/dot_general | solution.py:314
  82.3 45.0 %shard_map.60 = f32[8,3456]{1,0:T(8,128)} custom-call(f32[256,3456]{1,0:T(8,128)} %convolution_bitcast_fusion.terms_ref), custom_call_target="tpu_custom_call" | custom-call | flops 884736 | bytes 7077888 | tf_op jit(solution)/shard_map/pallas_call | solution.py:127
  127.2 1.2 reshape.91
  128.9 1.1 reshape.96
  130.0 6.9 %all-to-all-start.4 = ((f32[8,1,3456]{2,1,0:T(1,128)}), f32[8,1,3456]{2,1,0:T(1,128)S(1)}, u32[]{:S(2)}, u32[]{:S(2)}) async-start(f32[8,1,3456]{2,1,0:T(1,128)} %reshape.96), calls=%async_computation.4 | async-start | bytes 221184 | tf_op jit(solution)/shard_map/all_to_all | solution.py:322
  136.9 2.5 %convolution_bitcast_fusion.1 = f32[1,3,6,24,27,128]{5,3,4,2,1,0:T(8,128)S(1)} fusion(bf16[3,6,24,256,1]{3,2,4,1,0:T(8,128)(2,1)S(1)} %bitcast.194, bf16[27,128,256,1,1]{2,1,0,4,3:T(8,128)(2,1)} %bitcast.189), kind=kOutput, calls=%fused_computation.10 | convolution fusion | flops 764411904 | bytes 7962624 | tf_op jit(solution)/shard_map/dot_general | solution.py:232
  144.3 1.5 copy.243
  145.7 1.5 copy-done
  147.3 0.9 slice.189
  148.2 1.3 collective-permute-start.3
  149.5 1.0 fusion.8
  150.6 1.0 reshape.81
  152.0 2.2 %reshape.82 = bf16[8,2,6912]{2,1,0:T(2,128)(2,1)} reshape(bf16[8,4,8,3,6,24]{5,4,3,2,1,0:T(8,128)(2,1)S(1)} %copy.209) | data formatting | bytes 442368 | tf_op jit(solution)/shard_map/reshape | solution.py:170
  154.2 5.1 %all-to-all-start = ((bf16[8,2,6912]{2,1,0:T(2,128)(2,1)}), bf16[8,2,6912]{2,1,0:T(2,128)(2,1)S(1)}, u32[]{:S(2)}, u32[]{:S(2)}) async-start(bf16[8,2,6912]{2,1,0:T(2,128)(2,1)} %reshape.82), calls=%async_computation | async-start | bytes 442368 | tf_op jit(solution)/shard_map/all_to_all | solution.py:170
  159.8 0.9 reduce
  161.1 2.0 slice.187
  163.1 1.8 all-to-all-done
  164.9 1.0 reshape_reshape_reshape.6
  165.9 22.0 %all-to-all-start.1 = ((bf16[32,2,1728]{2,1,0:T(2,128)(2,1)}), bf16[32,2,1728]{2,1,0:T(2,128)(2,1)}, u32[]{:S(2)}, u32[]{:S(2)}) async-start(bf16[32,2,1728]{2,1,0:T(2,128)(2,1)} %reshape_reshape_reshape.6), calls=%async_computation.1 | async-start | bytes 458752 | tf_op jit(solution)/shard_map/all_to_all | solution.py:170
  187.9 2.3 %slice_add_fusion = f32[1,1,13,49,128]{4,1,3,2,0:T(1,128)S(1)} fusion(f32[1,1,13,49,128]{4,1,3,2,0:T(1,128)} %collective-permute-done.3, f32[1,8,14,50,128]{4,1,3,2,0:T(8,128)} %bitcast.171), kind=kLoop, calls=%fused_computation.32 | loop fusion | flops 81536 | bytes 978432 | tf_op jit(solution)/shard_map/add | solution.py:327
  190.8 1.1 copy-done.2
  192.5 1.3 collective-permute-start.4
  193.8 0.8 copy.249
  194.6 4.7 %collective-permute-done.4 = bf16[1,6,1,49,128]{4,1,3,2,0:T(8,128)(2,1)} collective-permute-done((bf16[1,6,1,49,128]{4,1,3,2,0:T(8,128)(2,1)}, bf16[1,6,1,49,128]{4,1,3,2,0:T(8,128)(2,1)}, u32[]{:S(2)}, u32[]{:S(2)}) %collective-permute-start.4) | collective-permute-done | bytes 75296 | tf_op jit(solution)/shard_map/ppermute | solution.py:177
  199.3 1.0 fusion.11
  200.6 1.0 copy.250
  201.6 2.9 %reshape_reshape.9 = bf16[8,4,8,3,6,24]{5,4,3,2,1,0:T(8,128)(2,1)S(1)} reshape(bf16[32,2,1728]{2,1,0:T(2,128)(2,1)} %all-to-all-done.1) | data formatting | bytes 442368 | tf_op jit(solution)/shard_map/reshape;reshape | solution.py:300
  204.9 2.6 %reshape.83 = bf16[1,8,24,576]{3,2,1,0:T(8,128)(2,1)} reshape(bf16[8,8,3,4,6,24]{5,4,3,2,1,0:T(8,128)(2,1)S(1)} %copy.210) | data formatting | bytes 442368 | tf_op jit(solution)/shard_map/reshape | solution.py:302
  (60 shorter events, 10.1 us)
Async XLA Ops:
  7.2 129.8 %all-gather.2.cloned.1.call-start = ((), (), s32[]{:S(2)}) async-start(), calls=%async_computation.5 | async-start | bytes 1990656 | tf_op jit(solution)/shard_map/all_gather | solution.py:268
  26.7 1.4 copy-start.5
  30.8 11.9 %copy-start.4 = (bf16[1,6,12,48,128]{4,3,2,1,0:T(8,128)(2,1)S(1)}, bf16[1,6,12,48,128]{4,3,2,1,0:T(8,128)(2,1)}, u32[]{:S(2)}) copy-start(bf16[1,6,12,48,128]{4,3,2,1,0:T(8,128)(2,1)} %param.3) | copy-start | bytes 2654212
  33.0 27.1 %all-to-all-start.2 = ((bf16[32,2,1728]{2,1,0:T(2,128)(2,1)}), bf16[32,2,1728]{2,1,0:T(2,128)(2,1)S(1)}, u32[]{:S(2)}, u32[]{:S(2)}) async-start(bf16[32,2,1728]{2,1,0:T(2,128)(2,1)} %reshape_reshape.10), calls=%async_computation.2 | async-start | bytes 458752 | tf_op jit(solution)/shard_map/all_to_all | solution.py:170
  42.7 24.1 %collective-permute-start.2 = (bf16[1,1,12,48,128]{4,3,2,1,0:T(8,128)(2,1)S(1)}, bf16[1,1,12,48,128]{4,3,2,1,0:T(8,128)(2,1)S(1)}, u32[]{:S(2)}, u32[]{:S(2)}) collective-permute-start(bf16[1,1,12,48,128]{4,3,2,1,0:T(8,128)(2,1)S(1)} %slice.125), channel_id=1, source_target_pairs={{0,32},{32,64},{64,96},{96,128},{128,160},{160,192},{192,224},{1,3... | collective-permute-start | bytes 442376 | tf_op jit(solution)/shard_map/ppermute | solution.py:177
  46.5 20.4 %collective-permute-start.1 = (bf16[1,6,1,48,128]{4,3,2,1,0:T(8,128)(2,1)S(1)}, bf16[1,6,1,48,128]{4,3,2,1,0:T(8,128)(2,1)S(1)}, u32[]{:S(2)}, u32[]{:S(2)}) collective-permute-start(bf16[1,6,1,48,128]{4,3,2,1,0:T(8,128)(2,1)S(1)} %slice.124), channel_id=1, source_target_pairs={{0,8},{8,16},{16,24},{1,9},{9,17},{17,25},{2,10},{10,18},{18,26},{... | collective-permute-start | bytes 221192 | tf_op jit(solution)/shard_map/ppermute | solution.py:177
  49.9 17.0 %collective-permute-start = (bf16[1,1,1,48,128]{4,3,2,1,0:T(8,128)(2,1)S(1)}, bf16[1,1,1,48,128]{4,3,2,1,0:T(8,128)(2,1)S(1)}, u32[]{:S(2)}, u32[]{:S(2)}) collective-permute-start(bf16[1,1,1,48,128]{4,3,2,1,0:T(8,128)(2,1)S(1)} %slice.123), channel_id=1, source_target_pairs={{0,40},{8,48},{16,56},{32,72},{40,80},{48,88},{64,104},{72,112},{8... | collective-permute-start | bytes 36872 | tf_op jit(solution)/shard_map/ppermute | solution.py:273
  61.1 12.4 %all-to-all-start.3 = ((bf16[8,2,6912]{2,1,0:T(2,128)(2,1)}), bf16[8,2,6912]{2,1,0:T(2,128)(2,1)S(1)}, u32[]{:S(2)}, u32[]{:S(2)}) async-start(bf16[8,2,6912]{2,1,0:T(2,128)(2,1)} %reshape_reshape_reshape.7), calls=%async_computation.3 | async-start | bytes 442368 | tf_op jit(solution)/shard_map/all_to_all | solution.py:170
  130.0 24.1 %all-to-all-start.4 = ((f32[8,1,3456]{2,1,0:T(1,128)}), f32[8,1,3456]{2,1,0:T(1,128)S(1)}, u32[]{:S(2)}, u32[]{:S(2)}) async-start(f32[8,1,3456]{2,1,0:T(1,128)} %reshape.96), calls=%async_computation.4 | async-start | bytes 221184 | tf_op jit(solution)/shard_map/all_to_all | solution.py:322
  144.2 5.2 %copy-start.1 = (bf16[3,6,24,3456]{3,2,1,0:T(8,128)(2,1)S(1)}, bf16[3,6,24,3456]{3,2,1,0:T(8,128)(2,1)}, u32[]{:S(2)}) copy-start(bf16[3,6,24,3456]{3,2,1,0:T(8,128)(2,1)} %shard_map.58) | copy-start | bytes 8957956
  144.2 5.2 %copy-start.3 = (bf16[3,3,3,128,256]{4,3,2,1,0:T(8,128)(2,1)S(1)}, bf16[3,3,3,128,256]{4,3,2,1,0:T(8,128)(2,1)}, u32[]{:S(2)}) copy-start(bf16[3,3,3,128,256]{4,3,2,1,0:T(8,128)(2,1)} %all-gather.2.cloned.1.call-done) | copy-start | bytes 5308420
  145.7 1.6 copy-start
  148.2 39.7 %collective-permute-start.3 = (f32[1,1,13,49,128]{4,1,3,2,0:T(1,128)}, f32[1,1,13,49,128]{4,1,3,2,0:T(1,128)}, u32[]{:S(2)}, u32[]{:S(2)}) collective-permute-start(f32[1,1,13,49,128]{4,1,3,2,0:T(1,128)} %slice.189), channel_id=1, source_target_pairs={{32,0},{64,32},{96,64},{128,96},{160,128},{192,160},{224,192},{33,... | collective-permute-start | bytes 978440 | tf_op jit(solution)/shard_map/ppermute | solution.py:177
  154.2 10.7 %all-to-all-start = ((bf16[8,2,6912]{2,1,0:T(2,128)(2,1)}), bf16[8,2,6912]{2,1,0:T(2,128)(2,1)S(1)}, u32[]{:S(2)}, u32[]{:S(2)}) async-start(bf16[8,2,6912]{2,1,0:T(2,128)(2,1)} %reshape.82), calls=%async_computation | async-start | bytes 442368 | tf_op jit(solution)/shard_map/all_to_all | solution.py:170
  165.9 35.7 %all-to-all-start.1 = ((bf16[32,2,1728]{2,1,0:T(2,128)(2,1)}), bf16[32,2,1728]{2,1,0:T(2,128)(2,1)}, u32[]{:S(2)}, u32[]{:S(2)}) async-start(bf16[32,2,1728]{2,1,0:T(2,128)(2,1)} %reshape_reshape_reshape.6), calls=%async_computation.1 | async-start | bytes 458752 | tf_op jit(solution)/shard_map/all_to_all | solution.py:170
  190.8 1.1 copy-start.2
  192.5 6.8 %collective-permute-start.4 = (bf16[1,6,1,49,128]{4,1,3,2,0:T(8,128)(2,1)}, bf16[1,6,1,49,128]{4,1,3,2,0:T(8,128)(2,1)}, u32[]{:S(2)}, u32[]{:S(2)}) collective-permute-start(bf16[1,6,1,49,128]{4,1,3,2,0:T(8,128)(2,1)} %slice.193), channel_id=1, source_target_pairs={{8,0},{16,8},{24,16},{9,1},{17,9},{25,17},{10,2},{18,10},{26,18},{... | collective-permute-start | bytes 225800 | tf_op jit(solution)/shard_map/ppermute | solution.py:177
  194.6 5.7 %slice-start = ((bf16[1,6,13,49,128]{4,1,3,2,0:T(8,128)(2,1)}), bf16[1,6,11,49,128]{4,1,3,2,0:T(8,128)(2,1)S(1)}, s32[]{:S(2)}) async-start(bf16[1,6,13,49,128]{4,1,3,2,0:T(8,128)(2,1)} %copy-done.2), calls=%async_computation.6 | async-start | bytes 2207744 | tf_op jit(solution)/shard_map/slice | solution.py:333
Sparse Core Ops, SparseCore 0:
  28.2 79.3 all-gather.1
where the time goes:
time: 217 us; the launch traced here: 214 us
  Pallas kernels  63.4 us (29%)
  starting transfers between devices  63.3 us (29%)
  local copies, waits for them, and re-layouts  42.6 us (20%)
  between operations  14.6 us (7%)
  waiting for transfers between devices  12.6 us (6%)
  other arithmetic  9.63 us (4%)
  matrix products  8.17 us (4%)
    pallas_call x1, Pallas kernels, reduce_filters(): pl.pallas_call(functools.partial(_reduce_body, n_sy, n_af), out_shape=jax...  45 us
    all_to_all x4, starting transfers between devices, flat_all_to_all(): moved = lax.all_to_all(x.reshape(x.shape[0], 2, -1), axes, 0, 0, tiled=True)  42.5 us
    pallas_call x1, Pallas kernels, gather_filters(): pl.pallas_call(functools.partial(_gather_body, n_sy, n_af), out_shape=jax...  14.3 us
    ppermute x4, starting transfers between devices, from_behind(): lax.ppermute(value, axis, [(source, source + steps) for source in range(l...  9.63 us
    all_to_all x4, waiting for transfers between devices, flat_all_to_all(): moved = lax.all_to_all(x.reshape(x.shape[0], 2, -1), axes, 0, 0, tiled=True)  7.82 us
    all_to_all x1, starting transfers between devices, on_device(): kernel_grad = lax.all_to_all(by_filter, 'sx', 0, 0, tiled=True).sum(axis=0)  6.87 us
    unnamed x16, local copies, waits for them, and re-layouts  6.12 us
    ppermute x4, waiting for transfers between devices, from_behind(): lax.ppermute(value, axis, [(source, source + steps) for source in range(l...  4.73 us
  transfers between devices with their start and end apart: 11, of which 3 were waited for; matrix products, arithmetic and copies ran while one was open for 21% of the time, Pallas kernels for 23%

commit v1 on v0

--- a/solution.py
+++ b/solution.py
@@ -216,7 +216,7 @@
         out_shape=jax.ShapeDtypeStruct((depth, height, width, 27 * channels), classes.dtype),
         in_specs=[pl.BlockSpec(memory_space=pltpu.VMEM)],
         out_specs=pl.BlockSpec(memory_space=pltpu.VMEM),
-    )(classes.astype(jnp.float32))
+    )(classes)
 
 
 def weave(even_part, odd_part, axis):

time: 217 us -> 217 us (level)
  starting transfers between devices: 63.3 us -> 66.3 us
  Pallas kernels: 63.4 us -> 61.1 us
    all_to_all x1, starting transfers between devices: 6.87 us -> 9.7 us  [on_device(): kernel_grad = lax.all_to_all(by_filter, 'sx', 0, 0, tiled=True).sum(axis=0)]
  transfers between devices with their start and end apart: 11 -> 11, of which waited for: 3 -> 4; matrix products, arithmetic and copies ran while one was open for 21% -> 21% of each run, Pallas kernels for 23% -> 22%
where the time goes in v1:
time: 217 us; the launch traced here: 214 us
  starting transfers between devices  66.3 us (31%)
  Pallas kernels  61.1 us (28%)
  local copies, waits for them, and re-layouts  43.8 us (20%)
  between operations  14.6 us (7%)
  waiting for transfers between devices  12.7 us (6%)
  matrix products  8.18 us (4%)
  other arithmetic  7.69 us (4%)
    pallas_call x1, Pallas kernels, reduce_filters(): pl.pallas_call(functools.partial(_reduce_body, n_sy, n_af), out_shape=jax...  43.1 us
    all_to_all x4, starting transfers between devices, flat_all_to_all(): moved = lax.all_to_all(x.reshape(x.shape[0], 2, -1), axes, 0, 0, tiled=True)  42.6 us
    pallas_call x1, Pallas kernels, gather_filters(): pl.pallas_call(functools.partial(_gather_body, n_sy, n_af), out_shape=jax...  14.3 us
    all_to_all x1, starting transfers between devices, on_device(): kernel_grad = lax.all_to_all(by_filter, 'sx', 0, 0, tiled=True).sum(axis=0)  9.7 us
    ppermute x4, starting transfers between devices, from_behind(): lax.ppermute(value, axis, [(source, source + steps) for source in range(l...  9.63 us
    all_to_all x4, waiting for transfers between devices, flat_all_to_all(): moved = lax.all_to_all(x.reshape(x.shape[0], 2, -1), axes, 0, 0, tiled=True)  7.95 us
    unnamed x16, local copies, waits for them, and re-layouts  6.12 us
    ppermute x4, waiting for transfers between devices, from_behind(): lax.ppermute(value, axis, [(source, source + steps) for source in range(l...  4.73 us
  transfers between devices with their start and end apart: 11, of which 4 were waited for; matrix products, arithmetic and copies ran while one was open for 21% of the time, Pallas kernels for 22%

profile of v1, /device:TPU:8, one launch (start us, length us, event | category | flops | bytes accessed | tf_op | source)
XLA Modules:
  0.0 214.3 jit_solution(12483212993939112688)
XLA Ops:
  7.2 0.9 copy.204
  8.1 0.7 reshape.66.block_ref
  8.9 14.3 %shard_map.59 = bf16[32,27,128]{2,1,0:T(8,128)(2,1)} custom-call(bf16[27,128]{1,0:T(8,128)(2,1)} %reshape.66.block_ref), custom_call_target="tpu_custom_call" | custom-call | tf_op jit(solution)/shard_map/pallas_call | solution.py:154
  23.2 1.4 copy.205
  24.6 2.1 copy.206
  26.7 1.3 copy.207
  28.1 2.2 %reshape.73 = bf16[8,8,3,4,6,24]{5,4,3,2,1,0:T(8,128)(2,1)S(1)} reshape(bf16[1,8,24,576]{3,2,1,0:T(8,128)(2,1)S(1)} %copy-done.5) | data formatting | bytes 442368 | tf_op jit(solution)/shard_map/reshape | solution.py:305
  30.8 2.2 %reshape_reshape.10 = bf16[32,2,1728]{2,1,0:T(2,128)(2,1)} reshape(bf16[8,4,8,3,6,24]{5,4,3,2,1,0:T(8,128)(2,1)S(1)} %copy.211) | data formatting | bytes 442368 | tf_op jit(solution)/shard_map/reshape;reshape | solution.py:170
  33.0 9.7 %all-to-all-start.2 = ((bf16[32,2,1728]{2,1,0:T(2,128)(2,1)}), bf16[32,2,1728]{2,1,0:T(2,128)(2,1)S(1)}, u32[]{:S(2)}, u32[]{:S(2)}) async-start(bf16[32,2,1728]{2,1,0:T(2,128)(2,1)} %reshape_reshape.10), calls=%async_computation.2 | async-start | bytes 458752 | tf_op jit(solution)/shard_map/all_to_all | solution.py:170
  42.7 3.7 %collective-permute-start.2 = (bf16[1,1,12,48,128]{4,3,2,1,0:T(8,128)(2,1)S(1)}, bf16[1,1,12,48,128]{4,3,2,1,0:T(8,128)(2,1)S(1)}, u32[]{:S(2)}, u32[]{:S(2)}) collective-permute-start(bf16[1,1,12,48,128]{4,3,2,1,0:T(8,128)(2,1)S(1)} %slice.125), channel_id=1, source_target_pairs={{0,32},{32,64},{64,96},{96,128},{128,160},{160,192},{192,224},{1,3... | collective-permute-start | bytes 442376 | tf_op jit(solution)/shard_map/ppermute | solution.py:177
  46.5 3.4 %collective-permute-start.1 = (bf16[1,6,1,48,128]{4,3,2,1,0:T(8,128)(2,1)S(1)}, bf16[1,6,1,48,128]{4,3,2,1,0:T(8,128)(2,1)S(1)}, u32[]{:S(2)}, u32[]{:S(2)}) collective-permute-start(bf16[1,6,1,48,128]{4,3,2,1,0:T(8,128)(2,1)S(1)} %slice.124), channel_id=1, source_target_pairs={{0,8},{8,16},{16,24},{1,9},{9,17},{17,25},{2,10},{10,18},{18,26},{... | collective-permute-start | bytes 221192 | tf_op jit(solution)/shard_map/ppermute | solution.py:177
  49.9 4.3 %collective-permute-start = (bf16[1,1,1,48,128]{4,3,2,1,0:T(8,128)(2,1)S(1)}, bf16[1,1,1,48,128]{4,3,2,1,0:T(8,128)(2,1)S(1)}, u32[]{:S(2)}, u32[]{:S(2)}) collective-permute-start(bf16[1,1,1,48,128]{4,3,2,1,0:T(8,128)(2,1)S(1)} %slice.123), channel_id=1, source_target_pairs={{0,40},{8,48},{16,56},{32,72},{40,80},{48,88},{64,104},{72,112},{8... | collective-permute-start | bytes 36872 | tf_op jit(solution)/shard_map/ppermute | solution.py:273
  54.1 6.0 %all-to-all-done.2 = bf16[32,2,1728]{2,1,0:T(2,128)(2,1)S(1)} async-done(((bf16[32,2,1728]{2,1,0:T(2,128)(2,1)}), bf16[32,2,1728]{2,1,0:T(2,128)(2,1)S(1)}, u32[]{:S(2)}, u32[]{:S(2)}) %all-to-all-start.2) | async-done | bytes 221216 | tf_op jit(solution)/shard_map/all_to_all | solution.py:170
  60.1 1.0 reshape_reshape_reshape.7
  61.1 5.7 %all-to-all-start.3 = ((bf16[8,2,6912]{2,1,0:T(2,128)(2,1)}), bf16[8,2,6912]{2,1,0:T(2,128)(2,1)S(1)}, u32[]{:S(2)}, u32[]{:S(2)}) async-start(bf16[8,2,6912]{2,1,0:T(2,128)(2,1)} %reshape_reshape_reshape.7), calls=%async_computation.3 | async-start | bytes 442368 | tf_op jit(solution)/shard_map/all_to_all | solution.py:170
  67.4 1.3 pad.98
  68.7 3.7 %shard_map.58 = bf16[3,6,24,3456]{3,2,1,0:T(8,128)(2,1)} custom-call(bf16[1,4,2,7,2,50,128]{6,5,4,3,2,1,0:T(8,128)(2,1)} %bitcast.174), custom_call_target="tpu_custom_call" | custom-call | tf_op jit(solution)/shard_map/pallas_call | solution.py:214
  72.5 1.7 reshape.74
  74.5 0.9 reshape_reshape.11
  75.4 0.9 reshape.75
  76.5 4.7 %convolution_bitcast_fusion.terms_ref = f32[256,3456]{1,0:T(8,128)} fusion(bf16[256,432]{1,0:T(8,128)(2,1)S(1)} %bitcast.191, bf16[432,3456]{1,0:T(8,128)(2,1)} %bitcast.171), kind=kOutput, calls=%fused_computation | convolution fusion | flops 764411904 | bytes 6746112 | tf_op jit(solution)/shard_map/dot_general | solution.py:314
  81.2 43.1 %shard_map.60 = f32[8,3456]{1,0:T(8,128)} custom-call(f32[256,3456]{1,0:T(8,128)} %convolution_bitcast_fusion.terms_ref), custom_call_target="tpu_custom_call" | custom-call | flops 884736 | bytes 7077888 | tf_op jit(solution)/shard_map/pallas_call | solution.py:127
  124.3 1.2 reshape.80
  126.0 1.1 reshape.84
  127.1 9.7 %all-to-all-start.4 = ((f32[8,1,3456]{2,1,0:T(1,128)}), f32[8,1,3456]{2,1,0:T(1,128)S(1)}, u32[]{:S(2)}, u32[]{:S(2)}) async-start(f32[8,1,3456]{2,1,0:T(1,128)} %reshape.84), calls=%async_computation.4 | async-start | bytes 221184 | tf_op jit(solution)/shard_map/all_to_all | solution.py:322
  136.8 2.5 %convolution_bitcast_fusion.1 = f32[1,3,6,24,27,128]{5,3,4,2,1,0:T(8,128)S(1)} fusion(bf16[3,6,24,256,1]{3,2,4,1,0:T(8,128)(2,1)S(1)} %bitcast.193, bf16[27,128,256,1,1]{2,1,0,4,3:T(8,128)(2,1)} %bitcast.188), kind=kOutput, calls=%fused_computation.10 | convolution fusion | flops 764411904 | bytes 7962624 | tf_op jit(solution)/shard_map/dot_general | solution.py:232
  144.2 1.5 copy.243
  145.7 1.5 copy-done
  147.2 0.9 slice.189
  148.1 1.3 collective-permute-start.3
  149.4 1.0 fusion.8
  150.5 1.0 reshape.70
  151.9 2.2 %reshape.71 = bf16[8,2,6912]{2,1,0:T(2,128)(2,1)} reshape(bf16[8,4,8,3,6,24]{5,4,3,2,1,0:T(8,128)(2,1)S(1)} %copy.209) | data formatting | bytes 442368 | tf_op jit(solution)/shard_map/reshape | solution.py:170
  154.1 5.7 %all-to-all-start = ((bf16[8,2,6912]{2,1,0:T(2,128)(2,1)}), bf16[8,2,6912]{2,1,0:T(2,128)(2,1)S(1)}, u32[]{:S(2)}, u32[]{:S(2)}) async-start(bf16[8,2,6912]{2,1,0:T(2,128)(2,1)} %reshape.71), calls=%async_computation | async-start | bytes 442368 | tf_op jit(solution)/shard_map/all_to_all | solution.py:170
  160.3 0.9 reduce
  161.6 2.0 slice.187
  163.6 1.8 all-to-all-done
  165.4 1.0 reshape_reshape_reshape.6
  166.4 21.5 %all-to-all-start.1 = ((bf16[32,2,1728]{2,1,0:T(2,128)(2,1)}), bf16[32,2,1728]{2,1,0:T(2,128)(2,1)}, u32[]{:S(2)}, u32[]{:S(2)}) async-start(bf16[32,2,1728]{2,1,0:T(2,128)(2,1)} %reshape_reshape_reshape.6), calls=%async_computation.1 | async-start | bytes 458752 | tf_op jit(solution)/shard_map/all_to_all | solution.py:170
  187.9 2.3 %slice_add_fusion = f32[1,1,13,49,128]{4,1,3,2,0:T(1,128)S(1)} fusion(f32[1,1,13,49,128]{4,1,3,2,0:T(1,128)} %collective-permute-done.3, f32[1,8,14,50,128]{4,1,3,2,0:T(8,128)} %bitcast.170), kind=kLoop, calls=%fused_computation.32 | loop fusion | flops 81536 | bytes 978432 | tf_op jit(solution)/shard_map/add | solution.py:327
  190.8 1.1 copy-done.2
  192.5 1.3 collective-permute-start.4
  193.9 0.8 copy.249
  194.7 4.7 %collective-permute-done.4 = bf16[1,6,1,49,128]{4,1,3,2,0:T(8,128)(2,1)} collective-permute-done((bf16[1,6,1,49,128]{4,1,3,2,0:T(8,128)(2,1)}, bf16[1,6,1,49,128]{4,1,3,2,0:T(8,128)(2,1)}, u32[]{:S(2)}, u32[]{:S(2)}) %collective-permute-start.4) | collective-permute-done | bytes 75296 | tf_op jit(solution)/shard_map/ppermute | solution.py:177
  199.4 1.0 fusion.11
  200.6 1.0 copy.250
  201.6 2.9 %reshape_reshape.9 = bf16[8,4,8,3,6,24]{5,4,3,2,1,0:T(8,128)(2,1)S(1)} reshape(bf16[32,2,1728]{2,1,0:T(2,128)(2,1)} %all-to-all-done.1) | data formatting | bytes 442368 | tf_op jit(solution)/shard_map/reshape;reshape | solution.py:300
  204.9 2.6 %reshape.72 = bf16[1,8,24,576]{3,2,1,0:T(8,128)(2,1)} reshape(bf16[8,8,3,4,6,24]{5,4,3,2,1,0:T(8,128)(2,1)S(1)} %copy.210) | data formatting | bytes 442368 | tf_op jit(solution)/shard_map/reshape | solution.py:302
  (59 shorter events, 10.1 us)
Async XLA Ops:
  7.2 129.7 %all-gather.2.cloned.1.call-start = ((), (), s32[]{:S(2)}) async-start(), calls=%async_computation.5 | async-start | bytes 1990656 | tf_op jit(solution)/shard_map/all_gather | solution.py:268
  26.7 1.4 copy-start.5
  30.8 11.9 %copy-start.4 = (bf16[1,6,12,48,128]{4,3,2,1,0:T(8,128)(2,1)S(1)}, bf16[1,6,12,48,128]{4,3,2,1,0:T(8,128)(2,1)}, u32[]{:S(2)}) copy-start(bf16[1,6,12,48,128]{4,3,2,1,0:T(8,128)(2,1)} %param.3) | copy-start | bytes 2654212
  33.0 27.1 %all-to-all-start.2 = ((bf16[32,2,1728]{2,1,0:T(2,128)(2,1)}), bf16[32,2,1728]{2,1,0:T(2,128)(2,1)S(1)}, u32[]{:S(2)}, u32[]{:S(2)}) async-start(bf16[32,2,1728]{2,1,0:T(2,128)(2,1)} %reshape_reshape.10), calls=%async_computation.2 | async-start | bytes 458752 | tf_op jit(solution)/shard_map/all_to_all | solution.py:170
  42.7 24.1 %collective-permute-start.2 = (bf16[1,1,12,48,128]{4,3,2,1,0:T(8,128)(2,1)S(1)}, bf16[1,1,12,48,128]{4,3,2,1,0:T(8,128)(2,1)S(1)}, u32[]{:S(2)}, u32[]{:S(2)}) collective-permute-start(bf16[1,1,12,48,128]{4,3,2,1,0:T(8,128)(2,1)S(1)} %slice.125), channel_id=1, source_target_pairs={{0,32},{32,64},{64,96},{96,128},{128,160},{160,192},{192,224},{1,3... | collective-permute-start | bytes 442376 | tf_op jit(solution)/shard_map/ppermute | solution.py:177
  46.5 20.4 %collective-permute-start.1 = (bf16[1,6,1,48,128]{4,3,2,1,0:T(8,128)(2,1)S(1)}, bf16[1,6,1,48,128]{4,3,2,1,0:T(8,128)(2,1)S(1)}, u32[]{:S(2)}, u32[]{:S(2)}) collective-permute-start(bf16[1,6,1,48,128]{4,3,2,1,0:T(8,128)(2,1)S(1)} %slice.124), channel_id=1, source_target_pairs={{0,8},{8,16},{16,24},{1,9},{9,17},{17,25},{2,10},{10,18},{18,26},{... | collective-permute-start | bytes 221192 | tf_op jit(solution)/shard_map/ppermute | solution.py:177
  49.9 17.0 %collective-permute-start = (bf16[1,1,1,48,128]{4,3,2,1,0:T(8,128)(2,1)S(1)}, bf16[1,1,1,48,128]{4,3,2,1,0:T(8,128)(2,1)S(1)}, u32[]{:S(2)}, u32[]{:S(2)}) collective-permute-start(bf16[1,1,1,48,128]{4,3,2,1,0:T(8,128)(2,1)S(1)} %slice.123), channel_id=1, source_target_pairs={{0,40},{8,48},{16,56},{32,72},{40,80},{48,88},{64,104},{72,112},{8... | collective-permute-start | bytes 36872 | tf_op jit(solution)/shard_map/ppermute | solution.py:273
  61.1 11.4 %all-to-all-start.3 = ((bf16[8,2,6912]{2,1,0:T(2,128)(2,1)}), bf16[8,2,6912]{2,1,0:T(2,128)(2,1)S(1)}, u32[]{:S(2)}, u32[]{:S(2)}) async-start(bf16[8,2,6912]{2,1,0:T(2,128)(2,1)} %reshape_reshape_reshape.7), calls=%async_computation.3 | async-start | bytes 442368 | tf_op jit(solution)/shard_map/all_to_all | solution.py:170
  127.1 27.0 %all-to-all-start.4 = ((f32[8,1,3456]{2,1,0:T(1,128)}), f32[8,1,3456]{2,1,0:T(1,128)S(1)}, u32[]{:S(2)}, u32[]{:S(2)}) async-start(f32[8,1,3456]{2,1,0:T(1,128)} %reshape.84), calls=%async_computation.4 | async-start | bytes 221184 | tf_op jit(solution)/shard_map/all_to_all | solution.py:322
  144.2 5.2 %copy-start.1 = (bf16[3,6,24,3456]{3,2,1,0:T(8,128)(2,1)S(1)}, bf16[3,6,24,3456]{3,2,1,0:T(8,128)(2,1)}, u32[]{:S(2)}) copy-start(bf16[3,6,24,3456]{3,2,1,0:T(8,128)(2,1)} %shard_map.58) | copy-start | bytes 8957956
  144.2 5.2 %copy-start.3 = (bf16[3,3,3,128,256]{4,3,2,1,0:T(8,128)(2,1)S(1)}, bf16[3,3,3,128,256]{4,3,2,1,0:T(8,128)(2,1)}, u32[]{:S(2)}) copy-start(bf16[3,3,3,128,256]{4,3,2,1,0:T(8,128)(2,1)} %all-gather.2.cloned.1.call-done) | copy-start | bytes 5308420
  145.7 1.6 copy-start
  148.1 39.8 %collective-permute-start.3 = (f32[1,1,13,49,128]{4,1,3,2,0:T(1,128)}, f32[1,1,13,49,128]{4,1,3,2,0:T(1,128)}, u32[]{:S(2)}, u32[]{:S(2)}) collective-permute-start(f32[1,1,13,49,128]{4,1,3,2,0:T(1,128)} %slice.189), channel_id=1, source_target_pairs={{32,0},{64,32},{96,64},{128,96},{160,128},{192,160},{224,192},{33,... | collective-permute-start | bytes 978440 | tf_op jit(solution)/shard_map/ppermute | solution.py:177
  154.1 11.3 %all-to-all-start = ((bf16[8,2,6912]{2,1,0:T(2,128)(2,1)}), bf16[8,2,6912]{2,1,0:T(2,128)(2,1)S(1)}, u32[]{:S(2)}, u32[]{:S(2)}) async-start(bf16[8,2,6912]{2,1,0:T(2,128)(2,1)} %reshape.71), calls=%async_computation | async-start | bytes 442368 | tf_op jit(solution)/shard_map/all_to_all | solution.py:170
  166.4 35.2 %all-to-all-start.1 = ((bf16[32,2,1728]{2,1,0:T(2,128)(2,1)}), bf16[32,2,1728]{2,1,0:T(2,128)(2,1)}, u32[]{:S(2)}, u32[]{:S(2)}) async-start(bf16[32,2,1728]{2,1,0:T(2,128)(2,1)} %reshape_reshape_reshape.6), calls=%async_computation.1 | async-start | bytes 458752 | tf_op jit(solution)/shard_map/all_to_all | solution.py:170
  190.8 1.1 copy-start.2
  192.5 6.8 %collective-permute-start.4 = (bf16[1,6,1,49,128]{4,1,3,2,0:T(8,128)(2,1)}, bf16[1,6,1,49,128]{4,1,3,2,0:T(8,128)(2,1)}, u32[]{:S(2)}, u32[]{:S(2)}) collective-permute-start(bf16[1,6,1,49,128]{4,1,3,2,0:T(8,128)(2,1)} %slice.193), channel_id=1, source_target_pairs={{8,0},{16,8},{24,16},{9,1},{17,9},{25,17},{10,2},{18,10},{26,18},{... | collective-permute-start | bytes 225800 | tf_op jit(solution)/shard_map/ppermute | solution.py:177
  194.7 5.7 %slice-start = ((bf16[1,6,13,49,128]{4,1,3,2,0:T(8,128)(2,1)}), bf16[1,6,11,49,128]{4,1,3,2,0:T(8,128)(2,1)S(1)}, s32[]{:S(2)}) async-start(bf16[1,6,13,49,128]{4,1,3,2,0:T(8,128)(2,1)} %copy-done.2), calls=%async_computation.6 | async-start | bytes 2207744 | tf_op jit(solution)/shard_map/slice | solution.py:333
Sparse Core Ops, SparseCore 0:
  28.2 79.5 all-gather.1
